TPU v7x, 256 devices: a whole 4x4x8 slice. The times are simulated.
256 devices in a mesh: row: 32 (over x_lo, z, core), col: 8 (over y, x_hi).
Axes of the slice: x: 4 (x_hi: 2, x_lo: 2; x = x_hi * 2 + x_lo), y: 4, z: 8, core: 2. Of those that a mesh axis runs over, the one named last changes fastest.
Arguments:
- corr: float32 [2, 8192, 8192], P(None, 'row', 'col'), may hold values from -6 to 6
- slope_prev: float32 [2, 8192, 8192], P(None, 'row', 'col'), may hold values from -6 to 6
- kappa: float32 [8192], replicated, may hold values from 0.05 to 0.2
- detuning: float32 [8192], replicated, may hold values from -1 to 1
- pump: float32 [8192], replicated, may hold values from 0.5 to 2
- round_trip: float32 [2], replicated, may hold values from -0.6 to 0.6
Outputs:
- slope: float32 [2, 8192, 8192], P(None, 'row', 'col')
All inputs are finite; a program needn't handle non-finite values.
Results may differ from a plain program's by a relative error of at most 0.00005.
Values sent between devices are 32-bit elements; how exact they have to be, the bound alone decides.
No kernel may reach another device: no remote copies, remote signals or barrier semaphores. Data moves between devices by JAX's collectives and lax.ppermute only.
A program may use at most 64 MiB of HBM per device.

v0:
```python
import jax
import jax.numpy as jnp
from jax import lax
from jax.sharding import PartitionSpec as P


def carried_in(x, axis, combine, identity):
    devices, here = (lax.axis_size(axis), lax.axis_index(axis))
    everything = lax.all_gather(x, axis)
    start = jnp.broadcast_to(jnp.asarray(identity, x.dtype), x.shape)

    def lap(k, before):
        reached = k < here
        new = combine(before, everything[k])
        return jnp.where(reached, new, before)

    return lax.fori_loop(0, devices, lap, start)


def lower_table(width):
    above = lax.broadcasted_iota(jnp.int32, (width, width), 0)
    beside = lax.broadcasted_iota(jnp.int32, (width, width), 1)
    return (above > beside).astype(jnp.float32)


def rows_prefix(part):
    count = part.shape[1]
    width = min(128, count)
    blocks = part.reshape(2, count // width, width, part.shape[2])
    within = jnp.einsum(
        "ij,pbjc->pbic", lower_table(width), blocks, precision=lax.Precision.HIGHEST
    )
    sums = jnp.sum(blocks, axis=2)
    earlier = jnp.cumsum(sums, axis=1) - sums
    return ((within + earlier[:, :, None, :]).reshape(part.shape), jnp.sum(sums, axis=1))


def cols_prefix(part):
    count = part.shape[2]
    width = min(128, count)
    blocks = part.reshape(2, part.shape[1], count // width, width)
    within = jnp.einsum(
        "prbj,ij->prbi", blocks, lower_table(width), precision=lax.Precision.HIGHEST
    )
    sums = jnp.sum(blocks, axis=3)
    earlier = jnp.cumsum(sums, axis=2) - sums
    return ((within + earlier[:, :, :, None]).reshape(part.shape), jnp.sum(sums, axis=2))


def add_pair(earlier, later):
    return earlier + later


def shards(corr, slope_prev, kappa, detuning, pump, round_trip):
    rows = corr.shape[1]
    cols = corr.shape[2]
    row_start = lax.axis_index("row") * rows
    col_start = lax.axis_index("col") * cols
    kappa_rows = lax.dynamic_slice_in_dim(kappa, row_start, rows)
    kappa_cols = lax.dynamic_slice_in_dim(kappa, col_start, cols)
    detune_rows = lax.dynamic_slice_in_dim(detuning, row_start, rows)
    detune_cols = lax.dynamic_slice_in_dim(detuning, col_start, cols)
    pump_rows = lax.dynamic_slice_in_dim(pump, row_start, rows)
    rho_re = round_trip[0]
    rho_im = round_trip[1]
    section = corr + 0.25 * slope_prev
    upper = section * kappa_rows[None, :, None]
    weighted = section * kappa_cols[None, None, :]
    local_rows, own_rows = rows_prefix(upper)
    local_cols, own_cols = cols_prefix(weighted)
    dev_rows = carried_in(own_rows, "row", add_pair, jnp.zeros_like(own_rows))
    dev_cols = carried_in(own_cols, "col", add_pair, jnp.zeros_like(own_cols))
    later_rows = lax.psum(own_rows, "row") - dev_rows - own_rows
    later_cols = lax.psum(own_cols, "col") - dev_cols - own_cols
    before = local_rows + dev_rows[:, None, :]
    after = later_rows[:, None, :] + (own_rows[:, None, :] - local_rows - upper)
    turned = jnp.stack(
        [rho_re * after[0] - rho_im * after[1], rho_re * after[1] + rho_im * after[0]]
    )
    field_left = -kappa_rows[None, :, None] * (before + 0.5 * upper + turned)
    before = local_cols + dev_cols[:, :, None]
    after = later_cols[:, :, None] + (own_cols[:, :, None] - local_cols - weighted)
    turned = jnp.stack(
        [rho_re * after[0] + rho_im * after[1], rho_re * after[1] - rho_im * after[0]]
    )
    field_right = -kappa_cols[None, None, :] * (before + 0.5 * weighted + turned)
    gap = detune_cols[None, :] - detune_rows[:, None]
    spin = jnp.stack([-gap * section[1], gap * section[0]])
    global_rows = row_start + lax.broadcasted_iota(jnp.int32, (rows, cols), 0)
    global_cols = col_start + lax.broadcasted_iota(jnp.int32, (rows, cols), 1)
    source = jnp.where(global_rows == global_cols, pump_rows[:, None], 0.0)
    source = jnp.stack([source, jnp.zeros_like(source)])
    return field_left + field_right + spin + source


def solution(mesh):
    placed = (P(None, "row", "col"), P(None, "row", "col"), P(), P(), P(), P())
    return jax.shard_map(
        shards, mesh=mesh, in_specs=placed, out_specs=P(None, "row", "col"), check_vma=False
    )
```

profile of v0, /device:TPU:1, one launch (start us, length us, event | category | flops | bytes accessed | tf_op | source)
XLA Modules:
  0.0 175.6 jit_solution(7867016755998997292)
XLA Ops:
  0.0 0.7 fusion.19
  0.7 3.8 %fusion.20 = (f32[2,256]{1,0:T(2,128)S(1)}, f32[2,256,1024]{2,1,0:T(8,128)S(1)}, f32[2,256,1024]{2,1,0:T(8,128)}) fusion(f32[1024]{0:T(1024)S(1)} %get-tuple-element.214, f32[2,256,1024]{2,1,0:T(8,128)} %param.10, f32[2,256,1024]{2,1,0:T(8,128)} %param.11), kind=kLoop, calls=%fused_computation.41 | loop fusion | flops 2096640 | bytes 8394752 | tf_op jit(solution)/shard_map/reduce_sum | solution.py:47
  4.5 0.5 copy.16
  5.0 0.6 bitcast_reduce_fusion
  5.6 0.4 reduce_window_sum.23
  6.2 2.6 %fusion.11 = f32[2,256,8,128]{1,3,2,0:T(8,128)} fusion(f32[2,256,8]{1,2,0:T(8,128)S(1)} %copy.11, f32[2,256,1024]{2,1,0:T(8,128)S(1)} %get-tuple-element.216), kind=kOutput, calls=%fused_computation.20 | convolution fusion | flops 805847040 | bytes 4210688 | tf_op jit(solution)/shard_map/prbj,ij->prbi/dot_general | solution.py:42
  8.8 2.9 %copy.12 = f32[2,256,1024]{2,1,0:T(8,128)} copy(f32[2,256,1024]{1,2,0:T(8,128)} %bitcast.52) | data formatting | bytes 4194304 | tf_op jit(solution)/shard_map/reshape | solution.py:47
  11.6 26.4 %all-gather.3 = f32[8,2,256]{2,1,0:T(2,128)S(1)} all-gather(f32[1,2,256]{2,1,0:T(2,128)S(1)} %bitcast.55), channel_id=3, replica_groups=mesh['row'=32,'col'=8] {'col'}, dimensions={0}, use_global_device_ids=true | all-gather | bytes 18432 | tf_op jit(solution)/shard_map/all_gather | solution.py:9
  38.0 0.3 while.29
  38.3 19.5 %psum.15 = f32[2,256]{1,0:T(2,128)S(1)} all-reduce(f32[2,256]{1,0:T(2,128)S(1)} %get-tuple-element.215), channel_id=1, replica_groups=mesh['row'=32,'col'=8] {'col'}, use_global_device_ids=true, to_apply=%region_11.12 | all-reduce | flops 512 | bytes 4096 | tf_op jit(solution)/shard_map/psum | solution.py:74
  57.8 1.9 %subtract_add_fusion = f32[2,256,1024]{2,1,0:T(8,128)S(1)} fusion(f32[2,256,1024]{2,1,0:T(8,128)S(1)} %get-tuple-element.216, f32[2,256,1024]{2,1,0:T(8,128)} %copy.12, f32[2,256]{1,0:T(2,128)S(1)} %get-tuple-element.215, f32[2,256]{1,0:T(2,128)S(1)} %subtract_subtract_fusion.1), kind=kLoop, calls=%fused_computation.18 | loop fusion | flops 1572864 | bytes 6295552 | tf_op jit(solution)/shard_map/add | solution.py:82
  59.8 0.6 fusion.22
  60.4 2.5 %multiply_add_fusion.1 = (f32[1,256,1024]{2,1,0:T(8,128)S(1)}, f32[1,256,1024]{2,1,0:T(8,128)}) fusion(f32[2,256,1024]{2,1,0:T(8,128)S(1)} %subtract_add_fusion, f32[]{:T(128)} %bitcast.8, f32[]{:T(128)} %bitcast.6), kind=kLoop, calls=%fused_computation.26 | loop fusion | flops 1572864 | bytes 4194312 | tf_op jit(solution)/shard_map/add | solution.py:84
  63.0 0.8 fusion.18
  63.7 1.8 %fusion.21 = (f32[2,1024]{1,0:T(2,128)S(1)}, f32[2,256,1024]{2,1,0:T(8,128)S(1)}) fusion(f32[2,256,1024]{2,1,0:T(8,128)} %get-tuple-element.217, f32[256]{0:T(256)S(1)} %get-tuple-element.212), kind=kLoop, calls=%fused_computation.42 | loop fusion | flops 1046528 | bytes 4203520 | tf_op jit(solution)/shard_map/reduce_sum | solution.py:35
  65.6 46.4 %all-gather.2 = f32[32,2,1024]{2,1,0:T(2,128)S(1)} all-gather(f32[1,2,1024]{2,1,0:T(2,128)S(1)} %bitcast.54), channel_id=2, replica_groups=mesh['row'=32,'col'=8] {'row'}, dimensions={0}, use_global_device_ids=true | all-gather | bytes 270336 | tf_op jit(solution)/shard_map/all_gather | solution.py:9
  112.0 1.3 while.28
  113.3 53.5 %psum.14 = f32[2,1024]{1,0:T(2,128)S(1)} all-reduce(f32[2,1024]{1,0:T(2,128)S(1)} %get-tuple-element.218), channel_id=1, replica_groups=mesh['row'=32,'col'=8] {'row'}, use_global_device_ids=true, to_apply=%region_5.6 | all-reduce | flops 2048 | bytes 16384 | tf_op jit(solution)/shard_map/psum | solution.py:73
  167.1 1.4 convolution_add_fusion
  168.5 0.5 fusion.10
  169.0 1.7 multiply_subtract_fusion.1
  171.0 0.9 dynamic_slice.33
  172.4 0.6 copy-done.2
  173.3 2.3 %fusion.6 = f32[2,256,1024]{2,1,0:T(8,128)} fusion(f32[1,256,1024]{2,1,0:T(8,128)S(1)} %get-tuple-element.225, f32[1,256,1024]{2,1,0:T(8,128)S(1)} %get-tuple-element.224, f32[1,256,1024]{2,1,0:T(8,128)S(1)} %copy-done.4, f32[1,256,1024]{2,1,0:T(8,128)S(1)} %get-tuple-element.222, f32[1,256,1024]{2,1,0:T(8,128)S(1)} %get-tuple-element.221, ...), kind=kLoop, calls=%fused_computation.10 | loop fusion | flops 8388608 | bytes 17841152 | tf_op jit(solution)/shard_map/add | solution.py:93
  (69 shorter events, 2.1 us)
Async XLA Ops:
  4.5 53.3 %copy-start = (f32[2,256,1024]{2,1,0:T(8,128)}, f32[2,256,1024]{2,1,0:T(8,128)S(1)}, u32[]{:S(2)}) copy-start(f32[2,256,1024]{2,1,0:T(8,128)S(1)} %get-tuple-element.216) | copy-start | bytes 6291460
  57.8 1.9 %copy-start.6 = (f32[2]{0:T(128)S(1)}, f32[2]{0:T(128)}, u32[]{:S(2)}) copy-start(f32[2]{0:T(128)} %param.15) | copy-start | bytes 28
  168.9 1.7 copy-start.5
  168.9 1.8 %copy-start.3 = (f32[2,256,1024]{2,1,0:T(8,128)S(1)}, f32[2,256,1024]{2,1,0:T(8,128)}, u32[]{:S(2)}) copy-start(f32[2,256,1024]{2,1,0:T(8,128)} %get-tuple-element.217) | copy-start | bytes 6291460
  168.9 1.8 %dynamic-slice-start = ((f32[8192]{0:T(1024)}, s32[]{:T(128)}), f32[1024]{0:T(1024)S(1)}, s32[]{:S(2)}) async-start(f32[8192]{0:T(1024)} %param.13, s32[]{:T(128)} %select_n.63), calls=%async_computation | async-start | bytes 8704 | tf_op jit(solution)/shard_map/dynamic_slice | solution.py:62
  170.8 1.6 copy-start.1
  170.8 2.2 %copy-start.2 = (f32[2,256,1024]{2,1,0:T(8,128)S(1)}, f32[2,256,1024]{2,1,0:T(8,128)}, u32[]{:S(2)}) copy-start(f32[2,256,1024]{2,1,0:T(8,128)} %copy.12) | copy-start | bytes 6291460
  170.8 2.5 %copy-start.4 = (f32[1,256,1024]{2,1,0:T(8,128)S(1)}, f32[1,256,1024]{2,1,0:T(8,128)}, u32[]{:S(2)}) copy-start(f32[1,256,1024]{2,1,0:T(8,128)} %get-tuple-element.223) | copy-start | bytes 3145732
where the time goes:
time: 176 us
  blocking collectives  146 us (83%)
  other arithmetic  18.4 us (10%)
  local copies, waits for them, and re-layouts  6.32 us (4%)
  matrix products  3.93 us (2%)
    all_gather x2, blocking collectives, carried_in(): everything = lax.all_gather(x, axis)  72.8 us
    psum x1, blocking collectives, shards(): later_rows = lax.psum(own_rows, 'row') - dev_rows - own_rows  53.5 us
    psum x1, blocking collectives, shards(): later_cols = lax.psum(own_cols, 'col') - dev_cols - own_cols  19.5 us
    reduce_sum x1, other arithmetic, cols_prefix(): jnp.sum(sums, axis=2)  3.83 us

commit v1 on v0

--- a/solution.py
+++ b/solution.py
@@ -71,7 +71,7 @@
     dev_rows = carried_in(own_rows, "row", add_pair, jnp.zeros_like(own_rows))
     dev_cols = carried_in(own_cols, "col", add_pair, jnp.zeros_like(own_cols))
     later_rows = lax.psum(own_rows, "row") - dev_rows - own_rows
-    later_cols = lax.psum(own_cols, "col") - dev_cols - own_cols
+    later_cols = jnp.sum(lax.all_gather(own_cols, "col"), axis=0) - dev_cols - own_cols
     before = local_rows + dev_rows[:, None, :]
     after = later_rows[:, None, :] + (own_rows[:, None, :] - local_rows - upper)
     turned = jnp.stack(

time: 176 us -> 154 us (0.88)
  blocking collectives: 146 us -> 124 us
    psum x1 -> x0, blocking collectives: 19.5 us -> none  [shards(): later_cols = lax.psum(own_cols, 'col') - dev_cols - own_cols]
    all_gather x2, blocking collectives: 72.8 us -> 70.2 us  [carried_in(): everything = lax.all_gather(x, axis)]
where the time goes in v1:
time: 154 us
  blocking collectives  124 us (81%)
  other arithmetic  18.4 us (12%)
  local copies, waits for them, and re-layouts  6.32 us (4%)
  matrix products  3.93 us (3%)
    all_gather x2, blocking collectives, carried_in(): everything = lax.all_gather(x, axis)  70.2 us
    psum x1, blocking collectives, shards(): later_rows = lax.psum(own_rows, 'row') - dev_rows - own_rows  53.5 us
    reduce_sum x1, other arithmetic, cols_prefix(): jnp.sum(sums, axis=2)  3.83 us

profile of v1, /device:TPU:1, one launch (start us, length us, event | category | flops | bytes accessed | tf_op | source)
XLA Modules:
  0.0 153.5 jit_solution(11494048680140368194)
XLA Ops:
  0.0 0.7 fusion.19
  0.7 3.8 %fusion.20 = (f32[2,256]{1,0:T(2,128)S(1)}, f32[2,256,1024]{2,1,0:T(8,128)S(1)}, f32[2,256,1024]{2,1,0:T(8,128)}) fusion(f32[1024]{0:T(1024)S(1)} %get-tuple-element.214, f32[2,256,1024]{2,1,0:T(8,128)} %param.10, f32[2,256,1024]{2,1,0:T(8,128)} %param.11), kind=kLoop, calls=%fused_computation.41 | loop fusion | flops 2096640 | bytes 8394752 | tf_op jit(solution)/shard_map/reduce_sum | solution.py:47
  4.5 0.5 copy.16
  5.0 0.6 bitcast_reduce_fusion
  5.6 0.4 reduce_window_sum.23
  6.2 2.6 %fusion.11 = f32[2,256,8,128]{1,3,2,0:T(8,128)} fusion(f32[2,256,8]{1,2,0:T(8,128)S(1)} %copy.11, f32[2,256,1024]{2,1,0:T(8,128)S(1)} %get-tuple-element.216), kind=kOutput, calls=%fused_computation.20 | convolution fusion | flops 805847040 | bytes 4210688 | tf_op jit(solution)/shard_map/prbj,ij->prbi/dot_general | solution.py:42
  8.8 2.9 %copy.12 = f32[2,256,1024]{2,1,0:T(8,128)} copy(f32[2,256,1024]{1,2,0:T(8,128)} %bitcast.52) | data formatting | bytes 4194304 | tf_op jit(solution)/shard_map/reshape | solution.py:47
  11.6 26.4 %all-gather.3 = f32[8,2,256]{2,1,0:T(2,128)S(1)} all-gather(f32[1,2,256]{2,1,0:T(2,128)S(1)} %bitcast.55), channel_id=3, replica_groups=mesh['row'=32,'col'=8] {'col'}, dimensions={0}, use_global_device_ids=true | all-gather | bytes 18432 | tf_op jit(solution)/shard_map/all_gather | solution.py:9
  38.0 0.3 while.29
  38.4 1.9 %subtract_add_fusion = f32[2,256,1024]{2,1,0:T(8,128)S(1)} fusion(f32[2,256,1024]{2,1,0:T(8,128)S(1)} %get-tuple-element.216, f32[2,256,1024]{2,1,0:T(8,128)} %copy.12, f32[2,256]{1,0:T(2,128)S(1)} %get-tuple-element.215, f32[2,256]{1,0:T(2,128)S(1)} %subtract_subtract_fusion.1), kind=kLoop, calls=%fused_computation.18 | loop fusion | flops 1572864 | bytes 6295552 | tf_op jit(solution)/shard_map/add | solution.py:82
  40.3 0.6 fusion.22
  41.0 2.5 %multiply_add_fusion.1 = (f32[1,256,1024]{2,1,0:T(8,128)S(1)}, f32[1,256,1024]{2,1,0:T(8,128)}) fusion(f32[2,256,1024]{2,1,0:T(8,128)S(1)} %subtract_add_fusion, f32[]{:T(128)} %bitcast.8, f32[]{:T(128)} %bitcast.6), kind=kLoop, calls=%fused_computation.26 | loop fusion | flops 1572864 | bytes 4194312 | tf_op jit(solution)/shard_map/add | solution.py:84
  43.5 0.8 fusion.18
  44.2 1.8 %fusion.21 = (f32[2,1024]{1,0:T(2,128)S(1)}, f32[2,256,1024]{2,1,0:T(8,128)S(1)}) fusion(f32[2,256,1024]{2,1,0:T(8,128)} %get-tuple-element.217, f32[256]{0:T(256)S(1)} %get-tuple-element.212), kind=kLoop, calls=%fused_computation.42 | loop fusion | flops 1046528 | bytes 4203520 | tf_op jit(solution)/shard_map/reduce_sum | solution.py:35
  46.1 43.8 %all-gather.2 = f32[32,2,1024]{2,1,0:T(2,128)S(1)} all-gather(f32[1,2,1024]{2,1,0:T(2,128)S(1)} %bitcast.54), channel_id=2, replica_groups=mesh['row'=32,'col'=8] {'row'}, dimensions={0}, use_global_device_ids=true | all-gather | bytes 270336 | tf_op jit(solution)/shard_map/all_gather | solution.py:9
  89.9 1.3 while.28
  91.3 53.5 %psum.7 = f32[2,1024]{1,0:T(2,128)S(1)} all-reduce(f32[2,1024]{1,0:T(2,128)S(1)} %get-tuple-element.218), channel_id=1, replica_groups=mesh['row'=32,'col'=8] {'row'}, use_global_device_ids=true, to_apply=%region_5.6 | all-reduce | flops 2048 | bytes 16384 | tf_op jit(solution)/shard_map/psum | solution.py:73
  145.0 1.4 convolution_add_fusion
  146.4 0.5 fusion.10
  146.9 1.7 %multiply_subtract_fusion.1 = (f32[1,256,1024]{2,1,0:T(8,128)S(1)}, f32[1,256,1024]{2,1,0:T(8,128)S(1)}) fusion(f32[2,256,1024]{2,1,0:T(8,128)S(1)} %fusion.10, f32[]{:T(128)} %bitcast.8, f32[]{:T(128)} %bitcast.6), kind=kLoop, calls=%fused_computation.29 | loop fusion | flops 1572864 | bytes 4194312 | tf_op jit(solution)/shard_map/sub | solution.py:78
  149.0 0.9 dynamic_slice.33
  150.0 0.3 copy-done.1
  150.3 0.6 copy-done.2
  151.2 2.3 %fusion.6 = f32[2,256,1024]{2,1,0:T(8,128)} fusion(f32[1,256,1024]{2,1,0:T(8,128)S(1)} %get-tuple-element.225, f32[1,256,1024]{2,1,0:T(8,128)S(1)} %get-tuple-element.224, f32[1,256,1024]{2,1,0:T(8,128)S(1)} %copy-done.4, f32[1,256,1024]{2,1,0:T(8,128)S(1)} %get-tuple-element.222, f32[1,256,1024]{2,1,0:T(8,128)S(1)} %get-tuple-element.221, ...), kind=kLoop, calls=%fused_computation.10 | loop fusion | flops 8388608 | bytes 17841152 | tf_op jit(solution)/shard_map/add | solution.py:93
  (69 shorter events, 1.8 us)
Async XLA Ops:
  4.5 33.8 %copy-start = (f32[2,256,1024]{2,1,0:T(8,128)}, f32[2,256,1024]{2,1,0:T(8,128)S(1)}, u32[]{:S(2)}) copy-start(f32[2,256,1024]{2,1,0:T(8,128)S(1)} %get-tuple-element.216) | copy-start | bytes 6291460
  38.4 1.9 %copy-start.6 = (f32[2]{0:T(128)S(1)}, f32[2]{0:T(128)}, u32[]{:S(2)}) copy-start(f32[2]{0:T(128)} %param.15) | copy-start | bytes 28
  146.9 1.7 %copy-start.5 = (f32[8192]{0:T(1024)S(1)}, f32[8192]{0:T(1024)}, u32[]{:S(2)}) copy-start(f32[8192]{0:T(1024)} %param.13) | copy-start | bytes 98308
  146.9 1.8 %copy-start.3 = (f32[2,256,1024]{2,1,0:T(8,128)S(1)}, f32[2,256,1024]{2,1,0:T(8,128)}, u32[]{:S(2)}) copy-start(f32[2,256,1024]{2,1,0:T(8,128)} %get-tuple-element.217) | copy-start | bytes 6291460
  146.9 1.8 %dynamic-slice-start = ((f32[8192]{0:T(1024)}, s32[]{:T(128)}), f32[1024]{0:T(1024)S(1)}, s32[]{:S(2)}) async-start(f32[8192]{0:T(1024)} %param.13, s32[]{:T(128)} %select_n.63), calls=%async_computation | async-start | bytes 8704 | tf_op jit(solution)/shard_map/dynamic_slice | solution.py:62
  148.7 1.6 %copy-start.1 = (f32[2,256,1024]{2,1,0:T(8,128)S(1)}, f32[2,256,1024]{2,1,0:T(8,128)}, u32[]{:S(2)}) copy-start(f32[2,256,1024]{2,1,0:T(8,128)} %copy-done) | copy-start | bytes 6291460
  148.7 2.2 %copy-start.2 = (f32[2,256,1024]{2,1,0:T(8,128)S(1)}, f32[2,256,1024]{2,1,0:T(8,128)}, u32[]{:S(2)}) copy-start(f32[2,256,1024]{2,1,0:T(8,128)} %copy.12) | copy-start | bytes 6291460
  148.7 2.5 %copy-start.4 = (f32[1,256,1024]{2,1,0:T(8,128)S(1)}, f32[1,256,1024]{2,1,0:T(8,128)}, u32[]{:S(2)}) copy-start(f32[1,256,1024]{2,1,0:T(8,128)} %get-tuple-element.223) | copy-start | bytes 3145732
